TPU v7x, 32 devices: a whole 2x2x4 slice. The times are simulated.
32 devices in a mesh: seq: 8 (over y, x, core), head: 4 (over z).
Axes of the slice: x: 2, y: 2, z: 4, core: 2. Of those that a mesh axis runs over, the one named last changes fastest.
Arguments:
- queries: bfloat16 [2048, 4096], P(('seq', 'head')), may hold values from -10 to 10
- keys: bfloat16 [2048, 1024], P(('seq', 'head')), may hold values from -10 to 10
- block_pos: int32 [16], replicated, may hold values from 0 to 15, each once
- query_map: float32 [32, 128, 128], P('head'), may hold values from -4 to 4
- key_map: float32 [8, 128, 128], P('head'), may hold values from -4 to 4
Outputs:
- query_map_gradient: float32 [32, 128, 128], P('head')
- key_map_gradient: float32 [8, 128, 128], P('head')
Inputs may be any that keep to these rules, and one draw needn't show every extreme that they name: A permutation: stored block g (token rows g * 128 to (g + 1) * 128 - 1) holds position block block_pos[g]; position blocks below 8 form the first sequence, the others the second.
All inputs are finite; a program needn't handle non-finite values.
Results may differ from a plain program's by a relative error of at most 0.0021.
Values may be sent and summed in bfloat16 or wider, within the bound.
No kernel may reach another device: no remote copies, remote signals or barrier semaphores. Data moves between devices by JAX's collectives and lax.ppermute only.
A program may use at most 64 MiB of HBM per device.

v0:
```python
import math
import jax
import jax.numpy as jnp
from jax import lax
from jax.sharding import PartitionSpec as P

HEAD_SIZE = 128
BLK = 128
HIGHEST = lax.Precision.HIGHEST
NEG_FLOOR = -1e30


def softmax_pair(logits):
    return jnp.concatenate(
        [jax.nn.softmax(logits, axis=-1), jax.nn.softmax(-logits, axis=-1)], axis=-1
    )


def feature_grad(feature, upstream):
    half_width = feature.shape[-1] // 2
    positive, negative = (feature[..., :half_width], feature[..., half_width:])
    grad_positive, grad_negative = (upstream[..., :half_width], upstream[..., half_width:])
    first = positive * (grad_positive - jnp.sum(grad_positive * positive, axis=-1, keepdims=True))
    second = negative * (grad_negative - jnp.sum(grad_negative * negative, axis=-1, keepdims=True))
    return first - second


def row_places(row_index, block_pos, seq_count):
    stored = row_index // BLK
    lookup = stored[:, None] == jnp.arange(block_pos.shape[0], dtype=jnp.int32)[None, :]
    blocks = jnp.sum(jnp.where(lookup, block_pos[None, :], 0), axis=1)
    return (blocks // seq_count, blocks * BLK + row_index % BLK)


def over_blocks(running, portions, step_fn):
    row_count = portions[0].shape[1]
    step_rows = math.gcd(row_count, 512)

    def advance(number, inner_carry):
        slabs = tuple(
            (
                lax.dynamic_slice_in_dim(portion, number * step_rows, step_rows, 1)
                for portion in portions
            )
        )
        return step_fn(inner_carry, slabs, number * step_rows)

    return lax.fori_loop(0, row_count // step_rows, advance, running)


def per_device(queries, keys, block_pos, query_map, key_map):
    local_q, local_k = (
        lax.all_to_all(queries, "head", split_axis=1, concat_axis=0, tiled=True),
        lax.all_to_all(keys, "head", split_axis=1, concat_axis=0, tiled=True),
    )
    seq_count = lax.axis_size("seq")
    seq_rank = lax.axis_index("seq")
    rows_local = local_k.shape[0]
    token_count = rows_local * seq_count
    key_heads = key_map.shape[0]
    group_width = query_map.shape[0] // key_heads
    score_scale = HEAD_SIZE ** (-0.5)
    query_index = seq_rank * rows_local + jnp.arange(rows_local, dtype=jnp.int32)
    query_heads = local_q.reshape(rows_local, key_heads, group_width, HEAD_SIZE).transpose(
        1, 2, 0, 3
    )
    query_wide = query_heads.astype(jnp.float32)
    query_logits = jnp.einsum(
        "vgnd,vgde->vgne",
        query_wide,
        query_map.reshape(key_heads, group_width, HEAD_SIZE, HEAD_SIZE),
        precision=HIGHEST,
    )
    rows_all = group_width * rows_local
    phi_query = softmax_pair(query_logits).reshape(key_heads, rows_all, 2 * HEAD_SIZE)
    phi_query_b = phi_query.astype(jnp.bfloat16)
    query_flat = query_heads.reshape(key_heads, rows_all, HEAD_SIZE)
    query_seq, query_at = row_places(query_index, block_pos, seq_count)
    query_seq = jnp.tile(query_seq, group_width)
    query_at = jnp.tile(query_at, group_width)

    def visible_for(offset, slab_rows):
        key_index = offset + jnp.arange(slab_rows, dtype=jnp.int32)
        key_seq, key_at = row_places(key_index, block_pos, seq_count)
        return (key_seq[None, :] == query_seq[:, None]) & (key_at[None, :] <= query_at[:, None])

    def key_features(key_slab):
        logits = jnp.einsum(
            "vwd,vde->vwe", key_slab.astype(jnp.float32), key_map, precision=HIGHEST
        )
        return softmax_pair(logits)

    def teacher(key_slab):
        return (
            jnp.einsum("vrd,vwd->vrw", query_flat, key_slab, preferred_element_type=jnp.float32)
            * score_scale
        )

    def stats_step(running, slabs, offset):
        key_slab = slabs[0]
        visible = visible_for(offset, key_slab.shape[1])

        def stats_compute_live(current):
            highest, denominator, linear_sum = current
            masked = jnp.where(visible[None], teacher(key_slab), NEG_FLOOR)
            new_high = jnp.maximum(highest, jnp.max(masked, axis=-1))
            exponent = jnp.where(visible[None], jnp.exp(masked - new_high[..., None]), 0.0)
            denominator = denominator * jnp.exp(highest - new_high) + jnp.sum(exponent, axis=-1)
            phi_key_b = key_features(key_slab).astype(jnp.bfloat16)
            linear = jnp.einsum(
                "vrf,vwf->vrw", phi_query_b, phi_key_b, preferred_element_type=jnp.float32
            )
            linear_sum = linear_sum + jnp.sum(jnp.where(visible[None], linear, 0.0), axis=-1)
            return (new_high, denominator, linear_sum)

        return lax.cond(jnp.any(visible), stats_compute_live, lambda current: current, running)

    def grads_step(running, slabs, offset):
        key_slab = slabs[0]
        visible = visible_for(offset, key_slab.shape[1])

        def grads_compute_live(current):
            query_grad, key_weight_grad = current
            masked = jnp.where(visible[None], teacher(key_slab), NEG_FLOOR)
            exponent = jnp.where(visible[None], jnp.exp(masked - highest[..., None]), 0.0)
            teacher_prob = exponent / denominator[..., None]
            phi_key = key_features(key_slab)
            phi_key_b = phi_key.astype(jnp.bfloat16)
            linear = jnp.einsum(
                "vrf,vwf->vrw", phi_query_b, phi_key_b, preferred_element_type=jnp.float32
            )
            weights = (
                jnp.where(visible[None], 1.0 / linear_sum[..., None] - teacher_prob / linear, 0.0)
                / token_count
            ).astype(jnp.bfloat16)
            query_grad = query_grad + jnp.einsum(
                "vrw,vwf->vrf", weights, phi_key_b, preferred_element_type=jnp.float32
            )
            key_grad = jnp.einsum(
                "vrw,vrf->vwf", weights, phi_query_b, preferred_element_type=jnp.float32
            )
            key_logit_grad = feature_grad(phi_key, key_grad)
            key_weight_grad = key_weight_grad + jnp.einsum(
                "vwd,vwe->vde", key_slab.astype(jnp.float32), key_logit_grad, precision=HIGHEST
            )
            return (query_grad, key_weight_grad)

        return lax.cond(jnp.any(visible), grads_compute_live, lambda current: current, running)

    def as_heads(pieces):
        return pieces.reshape(pieces.shape[0], key_heads, -1).transpose(1, 0, 2)

    row_zeros = jnp.zeros((key_heads, rows_all), jnp.float32)
    stats_init = (jnp.full((key_heads, rows_all), NEG_FLOOR, jnp.float32), row_zeros, row_zeros)
    grads_init = (
        jnp.zeros((key_heads, rows_all, 2 * HEAD_SIZE), jnp.float32),
        jnp.zeros((key_heads, HEAD_SIZE, HEAD_SIZE), jnp.float32),
    )
    highest, denominator, linear_sum = over_blocks(
        stats_init, (as_heads(lax.all_gather(local_k, "seq", axis=0, tiled=True)),), stats_step
    )
    query_grad, key_weight_grad = over_blocks(
        grads_init, (as_heads(lax.all_gather(local_k, "seq", axis=0, tiled=True)),), grads_step
    )
    query_logit_grad = feature_grad(phi_query, query_grad).reshape(
        key_heads, group_width, rows_local, HEAD_SIZE
    )
    query_weight_grad = jnp.einsum(
        "vgnd,vgne->vgde", query_wide, query_logit_grad, precision=HIGHEST
    ).reshape(key_heads * group_width, HEAD_SIZE, HEAD_SIZE)
    query_map_gradient, key_map_gradient = lax.psum((query_weight_grad, key_weight_grad), "seq")
    return (query_map_gradient, key_map_gradient)


def solution(mesh):
    in_specs = (
        P(("seq", "head"), None),
        P(("seq", "head"), None),
        P(),
        P("head", None, None),
        P("head", None, None),
    )
    out_specs = (P("head", None, None), P("head", None, None))
    return jax.shard_map(
        per_device, mesh=mesh, in_specs=in_specs, out_specs=out_specs, check_vma=False
    )
```

profile of v0, /device:TPU:0, one launch (start us, length us, event | category | flops | bytes accessed | tf_op | source)
XLA Modules:
  0.0 218.9 jit_solution(3189689803761205006)
XLA Ops:
  7.2 1.6 copy.131
  8.8 6.3 %all-to-all-start.1 = ((bf16[64,4,256]{2,0,1:T(8,128)(2,1)}), bf16[64,4,256]{2,0,1:T(8,128)(2,1)S(1)}, u32[]{:S(2)}, u32[]{:S(2)}) async-start(bf16[64,4,256]{2,0,1:T(8,128)(2,1)} %bitcast.86), calls=%async_computation.1 | async-start | bytes 262144 | tf_op jit(solution)/shard_map/all_to_all | solution.py:54
  15.2 1.9 copy.130
  17.0 4.2 %all-to-all-done.1 = bf16[64,4,256]{2,0,1:T(8,128)(2,1)S(1)} async-done(((bf16[64,4,256]{2,0,1:T(8,128)(2,1)}), bf16[64,4,256]{2,0,1:T(8,128)(2,1)S(1)}, u32[]{:S(2)}, u32[]{:S(2)}) %all-to-all-start.1) | async-done | bytes 131104 | tf_op jit(solution)/shard_map/all_to_all | solution.py:54
  21.2 3.5 %all-to-all-start = ((bf16[64,4,1024]{2,0,1:T(8,128)(2,1)}), bf16[64,4,1024]{2,0,1:T(8,128)(2,1)S(1)}, u32[]{:S(2)}, u32[]{:S(2)}) async-start(bf16[64,4,1024]{2,0,1:T(8,128)(2,1)} %bitcast.85), calls=%async_computation | async-start | bytes 1048576 | tf_op jit(solution)/shard_map/all_to_all | solution.py:53
  27.3 10.6 %all-to-all-done = bf16[64,4,1024]{2,0,1:T(8,128)(2,1)S(1)} async-done(((bf16[64,4,1024]{2,0,1:T(8,128)(2,1)}), bf16[64,4,1024]{2,0,1:T(8,128)(2,1)S(1)}, u32[]{:S(2)}, u32[]{:S(2)}) %all-to-all-start) | async-done | bytes 524320 | tf_op jit(solution)/shard_map/all_to_all | solution.py:53
  39.0 1.3 fusion.95
  40.3 1.3 fusion.93
  41.6 3.0 %pad_maximum_fusion.3 = f32[2,4,256,256]{2,3,1,0:T(8,128)} fusion(f32[2,4,256,128]{2,3,1,0:T(8,128)} %fusion.93, f32[2,4,256,128]{2,3,1,0:T(8,128)} %fusion.95), kind=kLoop, calls=%fused_computation.126 | loop fusion | flops 524288 | bytes 4194304 | tf_op jit(solution)/shard_map/concatenate | solution.py:14
  44.6 1.9 copy.94
  46.6 1.2 bitcast_convert_fusion
  47.8 2.3 %copy.101 = bf16[2,1024,256]{1,2,0:T(8,128)(2,1)} copy(bf16[2,1024,256]{2,1,0:T(8,128)(2,1)} %bitcast_convert_fusion) | data formatting | bytes 2097152
  50.0 2.8 %all-gather.2.cloned.1.call-done = bf16[2048,256]{1,0:T(8,128)(2,1)} async-done(((bf16[256,256]{1,0:T(8,128)(2,1)}), bf16[2048,256]{1,0:T(8,128)(2,1)}) %all-gather.2.cloned.1.call-update) | async-done | bytes 1048592 | tf_op jit(solution)/shard_map/all_gather | solution.py:163
  52.8 2.3 %copy.96 = bf16[2048,256]{0,1:T(8,128)(2,1)} copy(bf16[2048,256]{1,0:T(8,128)(2,1)} %all-gather.2.cloned.1.call-done) | data formatting | bytes 2097152 | tf_op jit(solution)/shard_map/all_gather | solution.py:163
  55.1 2.3 %copy.97 = bf16[2,2048,128]{2,1,0:T(8,128)(2,1)} copy(bf16[2,2048,128]{1,2,0:T(8,128)(2,1)} %bitcast.103) | data formatting | bytes 2097152
  57.4 28.7 %while.40 = (s32[]{:T(128)}, f32[2,1024]{1,0:T(2,128)S(1)}, f32[2,1024]{1,0:T(2,128)S(1)}, f32[2,1024]{1,0:T(2,128)S(1)}, s32[16]{0:T(128)S(1)}, /*index=5*/bf16...) while((s32[]{:T(128)}, f32[2,1024]{1,0:T(2,128)S(1)}, ...), condition=%wide.region_17.18_spmd.clone, body=%wide.region_5.17_spmd.clone.sunk | while | flops 1021495552 | bytes 21834140 | solution.py:48
  57.6 1.3 fusion.129
  59.5 6.8 %conditional.6 = ((f32[2,1024]{1,0:T(2,128)S(1)}, f32[2,1024]{1,0:T(2,128)S(1)}, f32[2,1024]{1,0:T(2,128)S(1)})) conditional(s32[]{:T(128)} %convert_element_type.44, (f32[2,1024]{1,0:T(2,128)S(1)}, f32[2,1024]{1,0:T(2,128)S(1)}, f32[2,1024]{1,0:T(2,128)S(1)}) %tuple.150, (pred[1024,512]{0,1:T(8,128)(4,1)S(1)}, s32[]{:T(128)}, ...), branch_computations={%region_8.8_spmd, %region_9.16_spmd} | conditional | flops 1019351296 | bytes 21258342 | solution.py:116
  59.5 1.4 fusion.20
  62.1 1.0 fusion.10
  63.1 2.0 fusion.11
  65.1 1.1 select_reduce_fusion
  66.4 1.3 fusion.129
  68.4 6.8 %conditional.6 = ((f32[2,1024]{1,0:T(2,128)S(1)}, f32[2,1024]{1,0:T(2,128)S(1)}, f32[2,1024]{1,0:T(2,128)S(1)})) conditional(s32[]{:T(128)} %convert_element_type.44, (f32[2,1024]{1,0:T(2,128)S(1)}, f32[2,1024]{1,0:T(2,128)S(1)}, f32[2,1024]{1,0:T(2,128)S(1)}) %tuple.150, (pred[1024,512]{0,1:T(8,128)(4,1)S(1)}, s32[]{:T(128)}, ...), branch_computations={%region_8.8_spmd, %region_9.16_spmd} | conditional | flops 1019351296 | bytes 21258342 | solution.py:116
  68.4 1.4 fusion.20
  71.0 1.0 fusion.10
  72.0 2.0 fusion.11
  74.0 1.1 select_reduce_fusion
  75.3 1.3 fusion.129
  77.2 6.8 %conditional.6 = ((f32[2,1024]{1,0:T(2,128)S(1)}, f32[2,1024]{1,0:T(2,128)S(1)}, f32[2,1024]{1,0:T(2,128)S(1)})) conditional(s32[]{:T(128)} %convert_element_type.44, (f32[2,1024]{1,0:T(2,128)S(1)}, f32[2,1024]{1,0:T(2,128)S(1)}, f32[2,1024]{1,0:T(2,128)S(1)}) %tuple.150, (pred[1024,512]{0,1:T(8,128)(4,1)S(1)}, s32[]{:T(128)}, ...), branch_computations={%region_8.8_spmd, %region_9.16_spmd} | conditional | flops 1019351296 | bytes 21258342 | solution.py:116
  77.3 1.4 fusion.20
  79.9 1.0 fusion.10
  80.9 2.0 fusion.11
  82.9 1.1 select_reduce_fusion
  84.2 1.3 fusion.129
  86.3 43.1 %while.41 = (s32[]{:T(128)}, f32[2,1024,256]{2,1,0:T(8,128)S(1)}, f32[2,128,128]{2,1,0:T(8,128)S(1)}, s32[16]{0:T(128)S(1)}, f32[2,1024]{1,0:T(2,128)S(1)}, /*in...) while((s32[]{:T(128)}, f32[2,1024,256]{2,1,0:T(8,128)S(1)}, ...), condition=%wide.region_29.30_spmd.clone, body=%wide.region_18.29_spmd.clone.sunk | while | flops 2299869440 | bytes 40643016 | solution.py:48
  86.5 1.9 fusion.130
  89.0 10.8 %conditional.7 = ((f32[2,1024,256]{2,1,0:T(8,128)S(1)}, f32[2,128,128]{2,1,0:T(8,128)S(1)})) conditional(s32[]{:T(128)} %convert_element_type.45, (f32[2,1024,256]{2,1,0:T(8,128)S(1)}, f32[2,128,128]{2,1,0:T(8,128)S(1)}) %tuple.156, (pred[1024,512]{0,1:T(8,128)(4,1)}, f32[2,1024]{1,0:T(2,128)S(1)}, s32[]{:T(128)}, ...), branch_computations={%region_21.21_spmd, %region_22.28_spmd} | conditional | flops 2297725184 | bytes 40067196 | solution.py:148
  89.0 1.3 fusion.51
  91.5 1.7 fusion.53
  93.2 2.5 %fusion.35 = bf16[2,1024,512]{1,2,0:T(8,128)(2,1)S(1)} fusion(f32[2,512,1024]{2,1,0:T(8,128)S(1)} %fusion.53, bf16[2,1024,256]{1,2,0:T(8,128)(2,1)S(1)} %copy-done.1, f32[2,1024]{1,0:T(2,128)S(1)} %get-tuple-element.811, f32[2,1024]{1,0:T(2,128)S(1)} %get-tuple-element.810, f32[2,1024]{1,0:T(2,128)S(1)} %broadcast_divide_fusion.2, ...), kind=kOutput, calls=%fused_computation.40 | convolution fusion | flops 548405248 | bytes 8413184 | tf_op jit(solution)/shard_map/while/body/eval_jaxpr/cond/branch_1_fun/vrf,vwf->vrw/dot_general | solution.py:129
  96.5 1.4 convolution_add_fusion
  98.2 1.6 convolution_add_fusion.1
  99.9 1.9 fusion.130
  102.4 10.8 %conditional.7 = ((f32[2,1024,256]{2,1,0:T(8,128)S(1)}, f32[2,128,128]{2,1,0:T(8,128)S(1)})) conditional(s32[]{:T(128)} %convert_element_type.45, (f32[2,1024,256]{2,1,0:T(8,128)S(1)}, f32[2,128,128]{2,1,0:T(8,128)S(1)}) %tuple.156, (pred[1024,512]{0,1:T(8,128)(4,1)}, f32[2,1024]{1,0:T(2,128)S(1)}, s32[]{:T(128)}, ...), branch_computations={%region_21.21_spmd, %region_22.28_spmd} | conditional | flops 2297725184 | bytes 40067196 | solution.py:148
  102.5 1.3 fusion.51
  105.0 1.7 fusion.53
  106.7 2.5 %fusion.35 = bf16[2,1024,512]{1,2,0:T(8,128)(2,1)S(1)} fusion(f32[2,512,1024]{2,1,0:T(8,128)S(1)} %fusion.53, bf16[2,1024,256]{1,2,0:T(8,128)(2,1)S(1)} %copy-done.1, f32[2,1024]{1,0:T(2,128)S(1)} %get-tuple-element.811, f32[2,1024]{1,0:T(2,128)S(1)} %get-tuple-element.810, f32[2,1024]{1,0:T(2,128)S(1)} %broadcast_divide_fusion.2, ...), kind=kOutput, calls=%fused_computation.40 | convolution fusion | flops 548405248 | bytes 8413184 | tf_op jit(solution)/shard_map/while/body/eval_jaxpr/cond/branch_1_fun/vrf,vwf->vrw/dot_general | solution.py:129
  109.9 1.4 convolution_add_fusion
  111.6 1.6 convolution_add_fusion.1
  113.4 1.9 fusion.130
  115.9 10.8 %conditional.7 = ((f32[2,1024,256]{2,1,0:T(8,128)S(1)}, f32[2,128,128]{2,1,0:T(8,128)S(1)})) conditional(s32[]{:T(128)} %convert_element_type.45, (f32[2,1024,256]{2,1,0:T(8,128)S(1)}, f32[2,128,128]{2,1,0:T(8,128)S(1)}) %tuple.156, (pred[1024,512]{0,1:T(8,128)(4,1)}, f32[2,1024]{1,0:T(2,128)S(1)}, s32[]{:T(128)}, ...), branch_computations={%region_21.21_spmd, %region_22.28_spmd} | conditional | flops 2297725184 | bytes 40067196 | solution.py:148
  115.9 1.3 fusion.51
  118.5 1.7 fusion.53
  120.1 2.5 %fusion.35 = bf16[2,1024,512]{1,2,0:T(8,128)(2,1)S(1)} fusion(f32[2,512,1024]{2,1,0:T(8,128)S(1)} %fusion.53, bf16[2,1024,256]{1,2,0:T(8,128)(2,1)S(1)} %copy-done.1, f32[2,1024]{1,0:T(2,128)S(1)} %get-tuple-element.811, f32[2,1024]{1,0:T(2,128)S(1)} %get-tuple-element.810, f32[2,1024]{1,0:T(2,128)S(1)} %broadcast_divide_fusion.2, ...), kind=kOutput, calls=%fused_computation.40 | convolution fusion | flops 548405248 | bytes 8413184 | tf_op jit(solution)/shard_map/while/body/eval_jaxpr/cond/branch_1_fun/vrf,vwf->vrw/dot_general | solution.py:129
  123.4 1.4 convolution_add_fusion
  125.1 1.6 convolution_add_fusion.1
  126.8 1.9 fusion.130
  129.4 2.0 fusion.86
  131.4 2.1 fusion.84
  133.5 1.1 fusion.88
  135.6 73.0 %all-reduce.3.cloned.1.call-done = (f32[8,128,128]{2,1,0:T(8,128)}, f32[2,128,128]{2,1,0:T(8,128)}) async-done(((f32[8,128,128]{2,1,0:T(8,128)}, f32[2,128,128]{2,1,0:T(8,128)}), (f32[8,128,128]{2,1,0:T(8,128)}, f32[2,128,128]{2,1,0:T(8,128)})) %all-reduce.3.cloned.1.call-update) | async-done | bytes 655376 | tf_op jit(solution)/shard_map/psum | solution.py:171
  208.6 1.9 copy.175
  210.5 1.6 copy.176
  (138 shorter events, 15.9 us)
Async XLA Ops:
  7.2 31.2 %copy-start = (f32[8,128,128]{2,1,0:T(8,128)S(1)}, f32[8,128,128]{2,1,0:T(8,128)}, u32[]{:S(2)}) copy-start(f32[8,128,128]{2,1,0:T(8,128)} %param.16) | copy-start | bytes 1572868
  8.8 12.4 %all-to-all-start.1 = ((bf16[64,4,256]{2,0,1:T(8,128)(2,1)}), bf16[64,4,256]{2,0,1:T(8,128)(2,1)S(1)}, u32[]{:S(2)}, u32[]{:S(2)}) async-start(bf16[64,4,256]{2,0,1:T(8,128)(2,1)} %bitcast.86), calls=%async_computation.1 | async-start | bytes 262144 | tf_op jit(solution)/shard_map/all_to_all | solution.py:54
  21.2 3.5 %copy-start.8 = (bf16[64,4,256]{2,0,1:T(8,128)(2,1)}, bf16[64,4,256]{2,0,1:T(8,128)(2,1)S(1)}, u32[]{:S(2)}) copy-start(bf16[64,4,256]{2,0,1:T(8,128)(2,1)S(1)} %all-to-all-done.1) | copy-start | bytes 393220
  21.2 16.7 %all-to-all-start = ((bf16[64,4,1024]{2,0,1:T(8,128)(2,1)}), bf16[64,4,1024]{2,0,1:T(8,128)(2,1)S(1)}, u32[]{:S(2)}, u32[]{:S(2)}) async-start(bf16[64,4,1024]{2,0,1:T(8,128)(2,1)} %bitcast.85), calls=%async_computation | async-start | bytes 1048576 | tf_op jit(solution)/shard_map/all_to_all | solution.py:53
  24.7 28.1 %all-gather.2.cloned.1.call-start = ((), (), s32[]{:S(2)}) async-start(), calls=%async_computation.2 | async-start | bytes 1179648 | tf_op jit(solution)/shard_map/all_gather | solution.py:163
  25.4 183.1 %all-reduce.3.cloned.1.call-start = ((), (), s32[]{:S(2)}) async-start(), calls=%async_computation.3 | async-start | bytes 1310720 | tf_op jit(solution)/shard_map/psum | solution.py:171
  38.3 3.3 %copy-start.4 = (bf16[256,2,4,128]{3,2,1,0:T(4,128)(2,1)}, bf16[256,2,4,128]{3,2,1,0:T(4,128)(2,1)S(1)}, u32[]{:S(2)}) copy-start(bf16[256,2,4,128]{3,2,1,0:T(4,128)(2,1)S(1)} %reshape.230) | copy-start | bytes 1572868
  46.5 10.8 %copy-start.2 = (f32[2,4,256,256]{3,2,1,0:T(8,128)}, f32[2,4,256,256]{3,2,1,0:T(8,128)S(1)}, u32[]{:S(2)}) copy-start(f32[2,4,256,256]{3,2,1,0:T(8,128)S(1)} %copy.94) | copy-start | bytes 6291460
  46.5 10.8 %copy-start.9 = (s32[16]{0:T(128)S(1)}, s32[16]{0:T(128)}, u32[]{:S(2)}) copy-start(s32[16]{0:T(128)} %param.15) | copy-start | bytes 196
  59.5 2.6 %copy-start.6 = (bf16[2,1024,256]{2,1,0:T(8,128)(2,1)S(1)}, bf16[2,1024,256]{2,1,0:T(8,128)(2,1)}, u32[]{:S(2)}) copy-start(bf16[2,1024,256]{2,1,0:T(8,128)(2,1)} %get-tuple-element.788) | copy-start | bytes 3145732 | tf_op jit(solution)/shard_map/while/body/eval_jaxpr/cond
  68.4 2.6 %copy-start.6 = (bf16[2,1024,256]{2,1,0:T(8,128)(2,1)S(1)}, bf16[2,1024,256]{2,1,0:T(8,128)(2,1)}, u32[]{:S(2)}) copy-start(bf16[2,1024,256]{2,1,0:T(8,128)(2,1)} %get-tuple-element.788) | copy-start | bytes 3145732 | tf_op jit(solution)/shard_map/while/body/eval_jaxpr/cond
  77.3 2.6 %copy-start.6 = (bf16[2,1024,256]{2,1,0:T(8,128)(2,1)S(1)}, bf16[2,1024,256]{2,1,0:T(8,128)(2,1)}, u32[]{:S(2)}) copy-start(bf16[2,1024,256]{2,1,0:T(8,128)(2,1)} %get-tuple-element.788) | copy-start | bytes 3145732 | tf_op jit(solution)/shard_map/while/body/eval_jaxpr/cond
  90.4 2.9 %copy-start.1 = (bf16[2,1024,256]{1,2,0:T(8,128)(2,1)S(1)}, bf16[2,1024,256]{1,2,0:T(8,128)(2,1)}, u32[]{:S(2)}) copy-start(bf16[2,1024,256]{1,2,0:T(8,128)(2,1)} %get-tuple-element.813) | copy-start | bytes 3145732 | tf_op jit(solution)/shard_map/while/body/eval_jaxpr/cond
  90.4 2.9 %copy-start.3 = (pred[1024,512]{0,1:T(8,128)(4,1)S(1)}, pred[1024,512]{0,1:T(8,128)(4,1)}, u32[]{:S(2)}) copy-start(pred[1024,512]{0,1:T(8,128)(4,1)} %get-tuple-element.805) | copy-start | bytes 1572868 | tf_op jit(solution)/shard_map/while/body/eval_jaxpr/cond
  103.8 2.9 %copy-start.1 = (bf16[2,1024,256]{1,2,0:T(8,128)(2,1)S(1)}, bf16[2,1024,256]{1,2,0:T(8,128)(2,1)}, u32[]{:S(2)}) copy-start(bf16[2,1024,256]{1,2,0:T(8,128)(2,1)} %get-tuple-element.813) | copy-start | bytes 3145732 | tf_op jit(solution)/shard_map/while/body/eval_jaxpr/cond
  103.8 2.9 %copy-start.3 = (pred[1024,512]{0,1:T(8,128)(4,1)S(1)}, pred[1024,512]{0,1:T(8,128)(4,1)}, u32[]{:S(2)}) copy-start(pred[1024,512]{0,1:T(8,128)(4,1)} %get-tuple-element.805) | copy-start | bytes 1572868 | tf_op jit(solution)/shard_map/while/body/eval_jaxpr/cond
  117.3 2.9 %copy-start.1 = (bf16[2,1024,256]{1,2,0:T(8,128)(2,1)S(1)}, bf16[2,1024,256]{1,2,0:T(8,128)(2,1)}, u32[]{:S(2)}) copy-start(bf16[2,1024,256]{1,2,0:T(8,128)(2,1)} %get-tuple-element.813) | copy-start | bytes 3145732 | tf_op jit(solution)/shard_map/while/body/eval_jaxpr/cond
  117.3 2.9 %copy-start.3 = (pred[1024,512]{0,1:T(8,128)(4,1)S(1)}, pred[1024,512]{0,1:T(8,128)(4,1)}, u32[]{:S(2)}) copy-start(pred[1024,512]{0,1:T(8,128)(4,1)} %get-tuple-element.805) | copy-start | bytes 1572868 | tf_op jit(solution)/shard_map/while/body/eval_jaxpr/cond
  129.4 5.2 %copy-start.7 = (f32[2,128,128]{2,1,0:T(8,128)}, f32[2,128,128]{2,1,0:T(8,128)S(1)}, u32[]{:S(2)}) copy-start(f32[2,128,128]{2,1,0:T(8,128)S(1)} %get-tuple-element.842) | copy-start | bytes 393220
  129.4 4.1 %copy-start.5 = (bf16[256,2,4,128]{3,2,1,0:T(4,128)(2,1)S(1)}, bf16[256,2,4,128]{3,2,1,0:T(4,128)(2,1)}, u32[]{:S(2)}) copy-start(bf16[256,2,4,128]{3,2,1,0:T(4,128)(2,1)} %copy-done.4) | copy-start | bytes 1572868
Sparse Core Ops, SparseCore 0:
  28.0 24.7 all-gather.1
  135.7 72.8 all-reduce.2
where the time goes:
time: 220 us; the launch traced here: 219 us
  waiting for transfers between devices  91.3 us (42%)
  matrix products  42.5 us (19%)
  other arithmetic  36.6 us (17%)
  local copies, waits for them, and re-layouts  18.5 us (8%)
  between operations  14.3 us (6%)
  starting transfers between devices  9.9 us (4%)
  loops' own time  5.95 us (3%)
    psum x1, waiting for transfers between devices, per_device(): lax.psum((query_weight_grad, key_weight_grad), 'seq')  73 us
    dot_general x6, matrix products, teacher(): jnp.einsum('vrd,vwd->vrw', query_flat, key_slab, preferred_element_type=j...  10.9 us
    all_to_all x1, waiting for transfers between devices, per_device(): lax.all_to_all(queries, 'head', split_axis=1, concat_axis=0, tiled=True)  10.6 us
    unnamed x19, local copies, waits for them, and re-layouts  9.04 us
    dot_general x6, matrix products, key_features(): jnp.einsum('vwd,vde->vwe', key_slab.astype(jnp.float32), key_map, precisi...  8.25 us
    reduce_or x4, other arithmetic, grads_step(): jnp.any(visible)  7.75 us
    dot_general x3, matrix products, grads_compute_live(): jnp.einsum('vrf,vwf->vrw', phi_query_b, phi_key_b, preferred_element_type...  7.47 us
    all_to_all x1, starting transfers between devices, per_device(): lax.all_to_all(keys, 'head', split_axis=1, concat_axis=0, tiled=True)  6.35 us
  transfers between devices with their start and end apart: 4, of which 4 were waited for; matrix products, arithmetic and copies ran while one was open for 7% of the time, Pallas kernels for 0%

commit v1 on v0

--- a/solution.py
+++ b/solution.py
@@ -3,11 +3,25 @@
 import jax.numpy as jnp
 from jax import lax
 from jax.sharding import PartitionSpec as P
+from jax.lax import axis_index, axis_size, ppermute
 
 HEAD_SIZE = 128
 BLK = 128
 HIGHEST = lax.Precision.HIGHEST
 NEG_FLOOR = -1e30
+
+
+def local_data_list(local_values, dim_k, u_in):
+    value_now, mat_out = (local_values.shape[:dim_k], local_values.shape[dim_k + 1 :])
+    after = jnp.moveaxis(local_values.reshape(*value_now, u_in, -1, *mat_out), dim_k, 0)
+    return after
+
+
+def hold_things(a0, ndim_at):
+    a0 = jnp.moveaxis(a0, 0, ndim_at)
+    odd = a0.shape
+    a_next = a0.reshape(*odd[:ndim_at], odd[ndim_at] * odd[ndim_at + 1], *odd[ndim_at + 2 :])
+    return a_next
 
 
 def softmax_pair(logits):
@@ -49,9 +63,24 @@
 
 
 def per_device(queries, keys, block_pos, query_map, key_map):
+
+    def _find_paths(z, link_axis, local_x, payload=0):
+        vec_out = axis_size(link_axis)
+        v_now = axis_index(link_axis)
+        carry, outer = (vec_out, v_now)
+        t_next = local_data_list(z, local_x, carry)
+        buffers = [t_next[outer]]
+        for b in [*range(1, carry)]:
+            earlier = t_next[outer ^ b]
+            kept_arr = ppermute(earlier, link_axis, [(q, q ^ b) for q in range(carry)])
+            buffers.append(kept_arr)
+        t_next = jnp.stack(buffers, 0)[outer ^ jnp.arange(carry)]
+        passed = hold_things(t_next, payload)
+        return passed
+
     local_q, local_k = (
         lax.all_to_all(queries, "head", split_axis=1, concat_axis=0, tiled=True),
-        lax.all_to_all(keys, "head", split_axis=1, concat_axis=0, tiled=True),
+        _find_paths(keys, "head", local_x=1),
     )
     seq_count = lax.axis_size("seq")
     seq_rank = lax.axis_index("seq")

time: 220 us -> 214 us (0.973)
  waiting for transfers between devices: 91.3 us -> 87.3 us
    all_to_all x1 -> x0, starting transfers between devices: 6.35 us -> none  [per_device(): lax.all_to_all(keys, 'head', split_axis=1, concat_axis=0, tiled=True)]
    ppermute x0 -> x3, starting transfers between devices: none -> 5.71 us  [_find_paths(): kept_arr = ppermute(earlier, link_axis, [(q, q ^ b) for q in range(carry)])]
    all_to_all x1 -> x0, waiting for transfers between devices: 4.2 us -> none  [per_device(): lax.all_to_all(keys, 'head', split_axis=1, concat_axis=0, tiled=True)]
    all_gather x1 -> x0, local copies, waits for them, and re-layouts: 2.28 us -> none  [per_device(): lax.all_gather(local_k, 'seq', axis=0, tiled=True)]
    unnamed x19 -> x23, local copies, waits for them, and re-layouts: 9.04 us -> 8.16 us
  transfers between devices with their start and end apart: 4 -> 6, of which waited for: 4 -> 3; matrix products, arithmetic and copies ran while one was open for 7% -> 7% of each run, Pallas kernels for 0% -> 0%
where the time goes in v1:
time: 214 us; the launch traced here: 213 us
  waiting for transfers between devices  87.3 us (41%)
  matrix products  42.5 us (20%)
  other arithmetic  35.9 us (17%)
  local copies, waits for them, and re-layouts  16.4 us (8%)
  between operations  14.4 us (7%)
  starting transfers between devices  10.8 us (5%)
  loops' own time  5.95 us (3%)
    psum x1, waiting for transfers between devices, per_device(): lax.psum((query_weight_grad, key_weight_grad), 'seq')  73 us
    all_to_all x1, waiting for transfers between devices, per_device(): lax.all_to_all(queries, 'head', split_axis=1, concat_axis=0, tiled=True)  11.9 us
    dot_general x6, matrix products, teacher(): jnp.einsum('vrd,vwd->vrw', query_flat, key_slab, preferred_element_type=j...  10.9 us
    dot_general x6, matrix products, key_features(): jnp.einsum('vwd,vde->vwe', key_slab.astype(jnp.float32), key_map, precisi...  8.25 us
    unnamed x23, local copies, waits for them, and re-layouts  8.16 us
    reduce_or x4, other arithmetic, grads_step(): jnp.any(visible)  7.75 us
    dot_general x3, matrix products, grads_compute_live(): jnp.einsum('vrf,vwf->vrw', phi_query_b, phi_key_b, preferred_element_type...  7.47 us
    ppermute x3, starting transfers between devices, _find_paths(): kept_arr = ppermute(earlier, link_axis, [(q, q ^ b) for q in range(carry)])  5.71 us
  transfers between devices with their start and end apart: 6, of which 3 were waited for; matrix products, arithmetic and copies ran while one was open for 7% of the time, Pallas kernels for 0%

profile of v1, /device:TPU:0, one launch (start us, length us, event | category | flops | bytes accessed | tf_op | source)
XLA Modules:
  0.0 213.3 jit_solution(18292937560824877490)
XLA Ops:
  7.2 1.0 reshape.259
  8.6 3.1 %collective-permute-start = (bf16[64,256]{1,0:T(8,128)(2,1)S(1)}, bf16[64,256]{1,0:T(8,128)(2,1)S(1)}, u32[]{:S(2)}, u32[]{:S(2)}) collective-permute-start(bf16[64,256]{1,0:T(8,128)(2,1)S(1)} %bitcast.125), channel_id=1, source_target_pairs={{0,1},{1,0},{2,3},{3,2},{4,5},{5,4},{6,7},{7,6},{8,9},{9,8},{10,11... | collective-permute-start | bytes 98312 | tf_op jit(solution)/shard_map/ppermute | solution.py:75
  11.7 2.6 %collective-permute-start.1 = (bf16[64,256]{1,0:T(8,128)(2,1)S(1)}, bf16[64,256]{1,0:T(8,128)(2,1)S(1)}, u32[]{:S(2)}, u32[]{:S(2)}) collective-permute-start(bf16[64,256]{1,0:T(8,128)(2,1)S(1)} %bitcast.126), channel_id=1, source_target_pairs={{0,2},{1,3},{2,0},{3,1},{4,6},{5,7},{6,4},{7,5},{8,10},{9,11},{10,... | collective-permute-start | bytes 98312 | tf_op jit(solution)/shard_map/ppermute | solution.py:75
  14.3 1.9 copy.113
  16.2 5.1 %all-to-all-start = ((bf16[64,4,1024]{2,0,1:T(8,128)(2,1)}), bf16[64,4,1024]{2,0,1:T(8,128)(2,1)S(1)}, u32[]{:S(2)}, u32[]{:S(2)}) async-start(bf16[64,4,1024]{2,0,1:T(8,128)(2,1)} %bitcast.93), calls=%async_computation | async-start | bytes 1048576 | tf_op jit(solution)/shard_map/all_to_all | solution.py:82
  23.0 11.9 %all-to-all-done = bf16[64,4,1024]{2,0,1:T(8,128)(2,1)S(1)} async-done(((bf16[64,4,1024]{2,0,1:T(8,128)(2,1)}), bf16[64,4,1024]{2,0,1:T(8,128)(2,1)S(1)}, u32[]{:S(2)}, u32[]{:S(2)}) %all-to-all-start) | async-done | bytes 524320 | tf_op jit(solution)/shard_map/all_to_all | solution.py:82
  36.0 1.3 fusion.95
  37.3 1.3 fusion.93
  38.6 3.0 %pad_maximum_fusion.3 = f32[2,4,256,256]{2,3,1,0:T(8,128)} fusion(f32[2,4,256,128]{2,3,1,0:T(8,128)} %fusion.93, f32[2,4,256,128]{2,3,1,0:T(8,128)} %fusion.95), kind=kLoop, calls=%fused_computation.127 | loop fusion | flops 524288 | bytes 4194304 | tf_op jit(solution)/shard_map/concatenate | solution.py:28
  41.6 2.0 copy.72
  43.6 1.2 bitcast_convert_fusion
  44.8 2.3 %copy.78 = bf16[2,1024,256]{1,2,0:T(8,128)(2,1)} copy(bf16[2,1024,256]{2,1,0:T(8,128)(2,1)} %bitcast_convert_fusion) | data formatting | bytes 2097152
  47.1 2.4 %all-gather.2.cloned.1.call-done = bf16[2048,256]{0,1:T(8,128)(2,1)} async-done(((bf16[256,256]{0,1:T(8,128)(2,1)}), bf16[2048,256]{0,1:T(8,128)(2,1)}) %all-gather.2.cloned.1.call-update) | async-done | bytes 1048592 | tf_op jit(solution)/shard_map/all_gather | solution.py:192
  49.5 2.3 %copy.74 = bf16[2,2048,128]{2,1,0:T(8,128)(2,1)} copy(bf16[2,2048,128]{1,2,0:T(8,128)(2,1)} %bitcast.117) | data formatting | bytes 2097152
  51.8 28.7 %while.40 = (s32[]{:T(128)}, f32[2,1024]{1,0:T(2,128)S(1)}, f32[2,1024]{1,0:T(2,128)S(1)}, f32[2,1024]{1,0:T(2,128)S(1)}, s32[16]{0:T(128)S(1)}, /*index=5*/bf16...) while((s32[]{:T(128)}, f32[2,1024]{1,0:T(2,128)S(1)}, ...), condition=%wide.region_17.18_spmd.clone, body=%wide.region_5.17_spmd.clone.sunk | while | flops 1021495552 | bytes 21834140 | solution.py:62
  52.0 1.3 fusion.130
  53.9 6.8 %conditional.6 = ((f32[2,1024]{1,0:T(2,128)S(1)}, f32[2,1024]{1,0:T(2,128)S(1)}, f32[2,1024]{1,0:T(2,128)S(1)})) conditional(s32[]{:T(128)} %convert_element_type.44, (f32[2,1024]{1,0:T(2,128)S(1)}, f32[2,1024]{1,0:T(2,128)S(1)}, f32[2,1024]{1,0:T(2,128)S(1)}) %tuple.151, (pred[1024,512]{0,1:T(8,128)(4,1)S(1)}, s32[]{:T(128)}, ...), branch_computations={%region_8.8_spmd, %region_9.16_spmd} | conditional | flops 1019351296 | bytes 21258342 | solution.py:145
  53.9 1.4 fusion.20
  56.5 1.0 fusion.10
  57.6 2.0 fusion.11
  59.5 1.1 select_reduce_fusion
  60.9 1.3 fusion.130
  62.8 6.8 %conditional.6 = ((f32[2,1024]{1,0:T(2,128)S(1)}, f32[2,1024]{1,0:T(2,128)S(1)}, f32[2,1024]{1,0:T(2,128)S(1)})) conditional(s32[]{:T(128)} %convert_element_type.44, (f32[2,1024]{1,0:T(2,128)S(1)}, f32[2,1024]{1,0:T(2,128)S(1)}, f32[2,1024]{1,0:T(2,128)S(1)}) %tuple.151, (pred[1024,512]{0,1:T(8,128)(4,1)S(1)}, s32[]{:T(128)}, ...), branch_computations={%region_8.8_spmd, %region_9.16_spmd} | conditional | flops 1019351296 | bytes 21258342 | solution.py:145
  62.8 1.4 fusion.20
  65.4 1.0 fusion.10
  66.4 2.0 fusion.11
  68.4 1.1 select_reduce_fusion
  69.7 1.3 fusion.130
  71.6 6.8 %conditional.6 = ((f32[2,1024]{1,0:T(2,128)S(1)}, f32[2,1024]{1,0:T(2,128)S(1)}, f32[2,1024]{1,0:T(2,128)S(1)})) conditional(s32[]{:T(128)} %convert_element_type.44, (f32[2,1024]{1,0:T(2,128)S(1)}, f32[2,1024]{1,0:T(2,128)S(1)}, f32[2,1024]{1,0:T(2,128)S(1)}) %tuple.151, (pred[1024,512]{0,1:T(8,128)(4,1)S(1)}, s32[]{:T(128)}, ...), branch_computations={%region_8.8_spmd, %region_9.16_spmd} | conditional | flops 1019351296 | bytes 21258342 | solution.py:145
  71.7 1.4 fusion.20
  74.3 1.0 fusion.10
  75.3 2.0 fusion.11
  77.3 1.1 select_reduce_fusion
  78.6 1.3 fusion.130
  80.7 43.1 %while.41 = (s32[]{:T(128)}, f32[2,1024,256]{2,1,0:T(8,128)S(1)}, f32[2,128,128]{2,1,0:T(8,128)S(1)}, s32[16]{0:T(128)S(1)}, f32[2,1024]{1,0:T(2,128)S(1)}, /*in...) while((s32[]{:T(128)}, f32[2,1024,256]{2,1,0:T(8,128)S(1)}, ...), condition=%wide.region_29.30_spmd.clone, body=%wide.region_18.29_spmd.clone.sunk | while | flops 2299869440 | bytes 40643016 | solution.py:62
  80.9 1.9 fusion.131
  83.4 10.8 %conditional.7 = ((f32[2,1024,256]{2,1,0:T(8,128)S(1)}, f32[2,128,128]{2,1,0:T(8,128)S(1)})) conditional(s32[]{:T(128)} %convert_element_type.45, (f32[2,1024,256]{2,1,0:T(8,128)S(1)}, f32[2,128,128]{2,1,0:T(8,128)S(1)}) %tuple.157, (pred[1024,512]{0,1:T(8,128)(4,1)}, f32[2,1024]{1,0:T(2,128)S(1)}, s32[]{:T(128)}, ...), branch_computations={%region_21.21_spmd, %region_22.28_spmd} | conditional | flops 2297725184 | bytes 40067196 | solution.py:177
  83.4 1.3 fusion.51
  85.9 1.7 fusion.53
  87.6 2.5 %fusion.35 = bf16[2,1024,512]{1,2,0:T(8,128)(2,1)S(1)} fusion(f32[2,512,1024]{2,1,0:T(8,128)S(1)} %fusion.53, bf16[2,1024,256]{1,2,0:T(8,128)(2,1)S(1)} %copy-done.1, f32[2,1024]{1,0:T(2,128)S(1)} %get-tuple-element.811, f32[2,1024]{1,0:T(2,128)S(1)} %get-tuple-element.810, f32[2,1024]{1,0:T(2,128)S(1)} %broadcast_divide_fusion.2, ...), kind=kOutput, calls=%fused_computation.41 | convolution fusion | flops 548405248 | bytes 8413184 | tf_op jit(solution)/shard_map/while/body/eval_jaxpr/cond/branch_1_fun/vrf,vwf->vrw/dot_general | solution.py:158
  90.9 1.4 convolution_add_fusion
  92.6 1.6 convolution_add_fusion.1
  94.3 1.9 fusion.131
  96.8 10.8 %conditional.7 = ((f32[2,1024,256]{2,1,0:T(8,128)S(1)}, f32[2,128,128]{2,1,0:T(8,128)S(1)})) conditional(s32[]{:T(128)} %convert_element_type.45, (f32[2,1024,256]{2,1,0:T(8,128)S(1)}, f32[2,128,128]{2,1,0:T(8,128)S(1)}) %tuple.157, (pred[1024,512]{0,1:T(8,128)(4,1)}, f32[2,1024]{1,0:T(2,128)S(1)}, s32[]{:T(128)}, ...), branch_computations={%region_21.21_spmd, %region_22.28_spmd} | conditional | flops 2297725184 | bytes 40067196 | solution.py:177
  96.9 1.3 fusion.51
  99.4 1.7 fusion.53
  101.1 2.5 %fusion.35 = bf16[2,1024,512]{1,2,0:T(8,128)(2,1)S(1)} fusion(f32[2,512,1024]{2,1,0:T(8,128)S(1)} %fusion.53, bf16[2,1024,256]{1,2,0:T(8,128)(2,1)S(1)} %copy-done.1, f32[2,1024]{1,0:T(2,128)S(1)} %get-tuple-element.811, f32[2,1024]{1,0:T(2,128)S(1)} %get-tuple-element.810, f32[2,1024]{1,0:T(2,128)S(1)} %broadcast_divide_fusion.2, ...), kind=kOutput, calls=%fused_computation.41 | convolution fusion | flops 548405248 | bytes 8413184 | tf_op jit(solution)/shard_map/while/body/eval_jaxpr/cond/branch_1_fun/vrf,vwf->vrw/dot_general | solution.py:158
  104.3 1.4 convolution_add_fusion
  106.0 1.6 convolution_add_fusion.1
  107.8 1.9 fusion.131
  110.3 10.8 %conditional.7 = ((f32[2,1024,256]{2,1,0:T(8,128)S(1)}, f32[2,128,128]{2,1,0:T(8,128)S(1)})) conditional(s32[]{:T(128)} %convert_element_type.45, (f32[2,1024,256]{2,1,0:T(8,128)S(1)}, f32[2,128,128]{2,1,0:T(8,128)S(1)}) %tuple.157, (pred[1024,512]{0,1:T(8,128)(4,1)}, f32[2,1024]{1,0:T(2,128)S(1)}, s32[]{:T(128)}, ...), branch_computations={%region_21.21_spmd, %region_22.28_spmd} | conditional | flops 2297725184 | bytes 40067196 | solution.py:177
  110.3 1.3 fusion.51
  112.9 1.7 fusion.53
  114.6 2.5 %fusion.35 = bf16[2,1024,512]{1,2,0:T(8,128)(2,1)S(1)} fusion(f32[2,512,1024]{2,1,0:T(8,128)S(1)} %fusion.53, bf16[2,1024,256]{1,2,0:T(8,128)(2,1)S(1)} %copy-done.1, f32[2,1024]{1,0:T(2,128)S(1)} %get-tuple-element.811, f32[2,1024]{1,0:T(2,128)S(1)} %get-tuple-element.810, f32[2,1024]{1,0:T(2,128)S(1)} %broadcast_divide_fusion.2, ...), kind=kOutput, calls=%fused_computation.41 | convolution fusion | flops 548405248 | bytes 8413184 | tf_op jit(solution)/shard_map/while/body/eval_jaxpr/cond/branch_1_fun/vrf,vwf->vrw/dot_general | solution.py:158
  117.8 1.4 convolution_add_fusion
  119.5 1.6 convolution_add_fusion.1
  121.3 1.9 fusion.131
  123.8 2.0 fusion.86
  125.8 2.1 fusion.84
  127.9 1.1 fusion.88
  129.0 1.0 copy.80
  130.0 73.0 %all-reduce.3.cloned.1.call-done = (f32[8,128,128]{2,1,0:T(8,128)}, f32[2,128,128]{2,1,0:T(8,128)}) async-done(((f32[8,128,128]{2,1,0:T(8,128)}, f32[2,128,128]{2,1,0:T(8,128)}), (f32[8,128,128]{2,1,0:T(8,128)}, f32[2,128,128]{2,1,0:T(8,128)})) %all-reduce.3.cloned.1.call-update) | async-done | bytes 655376 | tf_op jit(solution)/shard_map/psum | solution.py:200
  203.0 1.9 copy.161
  204.9 1.6 copy.162
  (151 shorter events, 14.3 us)
Async XLA Ops:
  7.2 28.2 %copy-start = (f32[8,128,128]{2,1,0:T(8,128)S(1)}, f32[8,128,128]{2,1,0:T(8,128)}, u32[]{:S(2)}) copy-start(f32[8,128,128]{2,1,0:T(8,128)} %param.16) | copy-start | bytes 1572868
  7.2 15.6 %copy-start.8 = (f32[2,128,128]{2,1,0:T(8,128)S(1)}, f32[2,128,128]{2,1,0:T(8,128)}, u32[]{:S(2)}) copy-start(f32[2,128,128]{2,1,0:T(8,128)} %param.17) | copy-start | bytes 393220
  7.2 15.7 %copy-start.9 = (s32[16]{0:T(128)S(1)}, s32[16]{0:T(128)}, u32[]{:S(2)}) copy-start(s32[16]{0:T(128)} %param.15) | copy-start | bytes 196
  8.6 12.7 %collective-permute-start = (bf16[64,256]{1,0:T(8,128)(2,1)S(1)}, bf16[64,256]{1,0:T(8,128)(2,1)S(1)}, u32[]{:S(2)}, u32[]{:S(2)}) collective-permute-start(bf16[64,256]{1,0:T(8,128)(2,1)S(1)} %bitcast.125), channel_id=1, source_target_pairs={{0,1},{1,0},{2,3},{3,2},{4,5},{5,4},{6,7},{7,6},{8,9},{9,8},{10,11... | collective-permute-start | bytes 98312 | tf_op jit(solution)/shard_map/ppermute | solution.py:75
  11.7 9.6 %collective-permute-start.1 = (bf16[64,256]{1,0:T(8,128)(2,1)S(1)}, bf16[64,256]{1,0:T(8,128)(2,1)S(1)}, u32[]{:S(2)}, u32[]{:S(2)}) collective-permute-start(bf16[64,256]{1,0:T(8,128)(2,1)S(1)} %bitcast.126), channel_id=1, source_target_pairs={{0,2},{1,3},{2,0},{3,1},{4,6},{5,7},{6,4},{7,5},{8,10},{9,11},{10,... | collective-permute-start | bytes 98312 | tf_op jit(solution)/shard_map/ppermute | solution.py:75
  14.3 7.0 %collective-permute-start.2 = (bf16[64,256]{1,0:T(8,128)(2,1)S(1)}, bf16[64,256]{1,0:T(8,128)(2,1)S(1)}, u32[]{:S(2)}, u32[]{:S(2)}) collective-permute-start(bf16[64,256]{1,0:T(8,128)(2,1)S(1)} %bitcast.127), channel_id=1, source_target_pairs={{0,3},{1,2},{2,1},{3,0},{4,7},{5,6},{6,5},{7,4},{8,11},{9,10},{10,... | collective-permute-start | bytes 98312 | tf_op jit(solution)/shard_map/ppermute | solution.py:75
  16.2 18.7 %all-to-all-start = ((bf16[64,4,1024]{2,0,1:T(8,128)(2,1)}), bf16[64,4,1024]{2,0,1:T(8,128)(2,1)S(1)}, u32[]{:S(2)}, u32[]{:S(2)}) async-start(bf16[64,4,1024]{2,0,1:T(8,128)(2,1)} %bitcast.93), calls=%async_computation | async-start | bytes 1048576 | tf_op jit(solution)/shard_map/all_to_all | solution.py:82
  21.3 28.2 %all-gather.2.cloned.1.call-start = ((), (), s32[]{:S(2)}) async-start(), calls=%async_computation.1 | async-start | bytes 1179648 | tf_op jit(solution)/shard_map/all_gather | solution.py:192
  22.7 180.3 %all-reduce.3.cloned.1.call-start = ((), (), s32[]{:S(2)}) async-start(), calls=%async_computation.2 | async-start | bytes 1310720 | tf_op jit(solution)/shard_map/psum | solution.py:200
  35.3 3.3 %copy-start.4 = (bf16[256,2,4,128]{3,2,1,0:T(4,128)(2,1)}, bf16[256,2,4,128]{3,2,1,0:T(4,128)(2,1)S(1)}, u32[]{:S(2)}) copy-start(bf16[256,2,4,128]{3,2,1,0:T(4,128)(2,1)S(1)} %reshape.256) | copy-start | bytes 1572868
  43.6 8.2 %copy-start.2 = (f32[2,4,256,256]{3,2,1,0:T(8,128)}, f32[2,4,256,256]{3,2,1,0:T(8,128)S(1)}, u32[]{:S(2)}) copy-start(f32[2,4,256,256]{3,2,1,0:T(8,128)S(1)} %copy.72) | copy-start | bytes 6291460
  53.9 2.6 %copy-start.6 = (bf16[2,1024,256]{2,1,0:T(8,128)(2,1)S(1)}, bf16[2,1024,256]{2,1,0:T(8,128)(2,1)}, u32[]{:S(2)}) copy-start(bf16[2,1024,256]{2,1,0:T(8,128)(2,1)} %get-tuple-element.788) | copy-start | bytes 3145732 | tf_op jit(solution)/shard_map/while/body/eval_jaxpr/cond
  62.8 2.6 %copy-start.6 = (bf16[2,1024,256]{2,1,0:T(8,128)(2,1)S(1)}, bf16[2,1024,256]{2,1,0:T(8,128)(2,1)}, u32[]{:S(2)}) copy-start(bf16[2,1024,256]{2,1,0:T(8,128)(2,1)} %get-tuple-element.788) | copy-start | bytes 3145732 | tf_op jit(solution)/shard_map/while/body/eval_jaxpr/cond
  71.7 2.6 %copy-start.6 = (bf16[2,1024,256]{2,1,0:T(8,128)(2,1)S(1)}, bf16[2,1024,256]{2,1,0:T(8,128)(2,1)}, u32[]{:S(2)}) copy-start(bf16[2,1024,256]{2,1,0:T(8,128)(2,1)} %get-tuple-element.788) | copy-start | bytes 3145732 | tf_op jit(solution)/shard_map/while/body/eval_jaxpr/cond
  84.8 2.9 %copy-start.1 = (bf16[2,1024,256]{1,2,0:T(8,128)(2,1)S(1)}, bf16[2,1024,256]{1,2,0:T(8,128)(2,1)}, u32[]{:S(2)}) copy-start(bf16[2,1024,256]{1,2,0:T(8,128)(2,1)} %get-tuple-element.813) | copy-start | bytes 3145732 | tf_op jit(solution)/shard_map/while/body/eval_jaxpr/cond
  84.8 2.9 %copy-start.3 = (pred[1024,512]{0,1:T(8,128)(4,1)S(1)}, pred[1024,512]{0,1:T(8,128)(4,1)}, u32[]{:S(2)}) copy-start(pred[1024,512]{0,1:T(8,128)(4,1)} %get-tuple-element.805) | copy-start | bytes 1572868 | tf_op jit(solution)/shard_map/while/body/eval_jaxpr/cond
  98.2 2.9 %copy-start.1 = (bf16[2,1024,256]{1,2,0:T(8,128)(2,1)S(1)}, bf16[2,1024,256]{1,2,0:T(8,128)(2,1)}, u32[]{:S(2)}) copy-start(bf16[2,1024,256]{1,2,0:T(8,128)(2,1)} %get-tuple-element.813) | copy-start | bytes 3145732 | tf_op jit(solution)/shard_map/while/body/eval_jaxpr/cond
  98.2 2.9 %copy-start.3 = (pred[1024,512]{0,1:T(8,128)(4,1)S(1)}, pred[1024,512]{0,1:T(8,128)(4,1)}, u32[]{:S(2)}) copy-start(pred[1024,512]{0,1:T(8,128)(4,1)} %get-tuple-element.805) | copy-start | bytes 1572868 | tf_op jit(solution)/shard_map/while/body/eval_jaxpr/cond
  111.7 2.9 %copy-start.1 = (bf16[2,1024,256]{1,2,0:T(8,128)(2,1)S(1)}, bf16[2,1024,256]{1,2,0:T(8,128)(2,1)}, u32[]{:S(2)}) copy-start(bf16[2,1024,256]{1,2,0:T(8,128)(2,1)} %get-tuple-element.813) | copy-start | bytes 3145732 | tf_op jit(solution)/shard_map/while/body/eval_jaxpr/cond
  111.7 2.9 %copy-start.3 = (pred[1024,512]{0,1:T(8,128)(4,1)S(1)}, pred[1024,512]{0,1:T(8,128)(4,1)}, u32[]{:S(2)}) copy-start(pred[1024,512]{0,1:T(8,128)(4,1)} %get-tuple-element.805) | copy-start | bytes 1572868 | tf_op jit(solution)/shard_map/while/body/eval_jaxpr/cond
  123.8 5.2 %copy-start.7 = (f32[2,128,128]{2,1,0:T(8,128)}, f32[2,128,128]{2,1,0:T(8,128)S(1)}, u32[]{:S(2)}) copy-start(f32[2,128,128]{2,1,0:T(8,128)S(1)} %get-tuple-element.842) | copy-start | bytes 393220
  123.8 4.1 %copy-start.5 = (bf16[256,2,4,128]{3,2,1,0:T(4,128)(2,1)S(1)}, bf16[256,2,4,128]{3,2,1,0:T(4,128)(2,1)}, u32[]{:S(2)}) copy-start(bf16[256,2,4,128]{3,2,1,0:T(4,128)(2,1)} %copy-done.4) | copy-start | bytes 1572868
Sparse Core Ops, SparseCore 0:
  24.5 24.9 all-gather.1
  130.1 72.8 all-reduce.2
